TPU v7x, 32 devices: a whole 2x2x4 slice. The times are simulated.
32 devices in a mesh: pix: 4 (over y, x), tm: 8 (over z, core).
Axes of the slice: x: 2, y: 2, z: 4, core: 2. Of those that a mesh axis runs over, the one named last changes fastest.
Arguments:
- movie: bfloat16 [80, 128, 1024], P('pix', None, 'tm'), may hold values from -6 to 6
- noise_weight: float32 [80, 128], P('pix'), may hold values from 0.25 to 4
- footprints: bfloat16 [80, 4, 128, 512], P('pix')
- block_ids: int32 [80, 4], P('pix'), may hold values from 0 to 31, as said below
- band_width: int32 [1024], replicated, may hold values from 0 to 5, as said below
- precision_blocks: bfloat16 [11, 128, 128], replicated
Outputs:
- traces: bfloat16 [16384, 1024], P('pix', 'tm')
- residual: bfloat16 [80, 128, 1024], P('pix', None, 'tm')
Inputs may be any that keep to these rules, and one draw needn't show every extreme that they name: `block_ids`: each tile names 4 different component blocks. `band_width`: some group has the reach 5.
All inputs are finite; a program needn't handle non-finite values.
Results may differ from a plain program's by a relative error of at most 0.015.
Values may be sent and summed in bfloat16 or wider, within the bound.
A program may use at most 128 MiB of HBM per device.

v0:
```python
import jax
import jax.numpy as jnp
from jax import lax
from jax.sharding import PartitionSpec as P

K = 16384
CBLK = 512
GROUP = 16
BMAX = 5
FR = 128


def dealt_groups(band_width, devices):
    ngroups = band_width.shape[0]
    expense = 2 * band_width + 1
    ranking = jnp.argsort(-expense, stable=True)
    position = jnp.arange(ngroups, dtype=jnp.int32)
    rounds = position // devices
    column = position % devices
    holder = jnp.where(rounds % 2 == 0, column, devices - 1 - column)
    target = holder * (ngroups // devices) + rounds
    return jnp.zeros((ngroups,), jnp.int32).at[target].set(ranking)


def group_widths(band_width, permuted, dev_rank, per_device):
    picked = lax.dynamic_slice_in_dim(permuted, dev_rank * per_device, per_device)
    matches = picked[:, None] == jnp.arange(band_width.shape[0], dtype=jnp.int32)[None, :]
    return jnp.sum(jnp.where(matches, band_width[None, :], 0), axis=1)


def band_filter(projected, widths, precision_blocks):
    row_count, frames = projected.shape
    local_groups = widths.shape[0]
    nblocks = frames // FR
    blocks = projected.reshape(local_groups, GROUP, nblocks, FR)
    padded = jnp.pad(blocks, ((0, 0), (0, 0), (BMAX, BMAX), (0, 0)))

    def one_group(member, output):
        band_reach = widths[member]
        source = lax.dynamic_index_in_dim(padded, member, 0, keepdims=False)

        def one_offset(step_index, running):
            offset = step_index - band_reach
            shifted = lax.dynamic_slice_in_dim(source, BMAX + offset, nblocks, 1)
            matrix = lax.dynamic_index_in_dim(precision_blocks, BMAX + offset, 0, keepdims=False)
            return running + jnp.einsum(
                "gbf,fh->gbh", shifted, matrix, preferred_element_type=jnp.float32
            )

        zero_block = jnp.zeros((GROUP, nblocks, FR), jnp.float32)
        result = lax.fori_loop(0, 2 * band_reach + 1, one_offset, zero_block)
        return lax.dynamic_update_index_in_dim(output, result, member, 0)

    blank_out = jnp.zeros((local_groups, GROUP, nblocks, FR), jnp.float32)
    filtered = lax.fori_loop(0, local_groups, one_group, blank_out)
    return filtered.reshape(row_count, frames)


def shards(movie, noise_weight, footprints, block_ids, band_width, precision_blocks):
    frames = movie.shape[2]
    comp_blocks = K // CBLK
    ngroups = K // GROUP
    pix_size = lax.axis_size("pix")
    tm_size = lax.axis_size("tm")
    per_device = ngroups // (pix_size * tm_size)
    weighted = (noise_weight[:, :, None] * movie.astype(jnp.float32)).astype(jnp.bfloat16)
    contrib = jnp.einsum("nspc,npf->nscf", footprints, weighted, preferred_element_type=jnp.float32)
    blank_sum = jnp.zeros((comp_blocks, CBLK, frames), jnp.float32)
    partial_value = (
        blank_sum.at[block_ids.reshape(-1)]
        .add(contrib.reshape(-1, CBLK, frames))
        .reshape(K, frames)
    )
    permuted = dealt_groups(band_width, pix_size * tm_size)
    partial_value = jnp.take(
        partial_value.reshape(ngroups, GROUP, frames), permuted, axis=0
    ).reshape(K, frames)
    moved = lax.all_to_all(
        partial_value.astype(jnp.bfloat16), "tm", split_axis=0, concat_axis=1, tiled=True
    )
    summed = lax.psum_scatter(
        moved.astype(jnp.float32).astype(jnp.bfloat16), "pix", scatter_dimension=0, tiled=True
    )
    dev_rank = lax.axis_index("tm") * pix_size + lax.axis_index("pix")
    widths = group_widths(band_width, permuted, dev_rank, per_device)
    traces_here = band_filter(summed, widths, precision_blocks).astype(jnp.bfloat16)
    collected = lax.all_gather(traces_here, "pix", axis=0, tiled=True)
    all_traces = lax.all_to_all(collected, "tm", split_axis=1, concat_axis=0, tiled=True)
    inverse = (
        jnp.zeros((ngroups,), jnp.int32).at[permuted].set(jnp.arange(ngroups, dtype=jnp.int32))
    )
    all_traces = jnp.take(all_traces.reshape(ngroups, GROUP, frames), inverse, axis=0).reshape(
        K, frames
    )
    shard_rows = K // pix_size
    traces_out = lax.dynamic_slice_in_dim(
        all_traces, lax.axis_index("pix") * shard_rows, shard_rows, 0
    )
    trace_blocks = all_traces.reshape(comp_blocks, CBLK, frames)
    chosen = jnp.take(trace_blocks, block_ids, axis=0)
    rebuilt = jnp.einsum("nspc,nscf->npf", footprints, chosen, preferred_element_type=jnp.float32)
    residual = (movie.astype(jnp.float32) - rebuilt).astype(jnp.bfloat16)
    return (traces_out, residual)


def solution(mesh):
    return jax.shard_map(
        shards,
        mesh=mesh,
        in_specs=(
            P("pix", None, "tm"),
            P("pix", None),
            P("pix", None, None, None),
            P("pix", None),
            P(),
            P(),
        ),
        out_specs=(P("pix", "tm"), P("pix", None, "tm")),
        check_vma=False,
    )
```

profile of v0, /device:TPU:0, one launch (start us, length us, event | category | flops | bytes accessed | tf_op | source)
XLA Modules:
  0.0 798.3 jit_solution(12882438811581009262)
XLA Ops:
  7.9 4.4 sort.17
  12.3 4.3 scatter_custom_fusion
  18.1 14.1 %fusion.17 = f32[20,128,4,512]{3,1,2,0:T(8,128)} fusion(bf16[20,4,128,512]{3,2,1,0:T(8,128)(2,1)} %param.12, bf16[20,128,128]{1,2,0:T(8,128)(2,1)S(1)} %copy.48, f32[20,128]{1,0:T(8,128)} %param.11), kind=kOutput, calls=%fused_computation.28 | convolution fusion | flops 1343160320 | bytes 32122880 | tf_op jit(solution)/shard_map/nspc,npf->nscf/dot_general | solution.py:67
  32.1 21.3 %copy.49 = f32[80,512,128]{2,1,0:T(8,128)} copy(f32[80,512,128]{1,2,0:T(8,128)} %bitcast.65) | data formatting | bytes 41943040 | tf_op jit(solution)/shard_map/reshape | solution.py:71
  54.2 4.3 broadcast_in_dim.103
  58.4 45.8 %scatter_fusion = f32[32,512,128]{2,1,0:T(8,128)} fusion(f32[32,512,128]{2,1,0:T(8,128)} %broadcast_in_dim.103, s32[80]{0:T(128)S(1)} %fusion.28, f32[80,512,128]{2,1,0:T(8,128)} %copy.49), kind=kCustom, calls=%fused_computation.5 | custom fusion | flops 5242880 | bytes 62914880 | tf_op jit(solution)/shard_map/scatter-add | solution.py:71
  104.2 11.9 %gather_fusion = bf16[1024,16,128]{2,1,0:T(8,128)(2,1)} fusion(f32[1024,16,128]{2,1,0:T(8,128)} %bitcast.64, s32[1024]{0:T(1024)S(1)} %get-tuple-element.264), kind=kCustom, calls=%fused_computation | custom fusion | bytes 8392704 | tf_op jit(solution)/shard_map/jit(_take)/gather | solution.py:75
  116.1 6.1 fusion.7
  122.2 100.2 %all_to_all.32 = bf16[8,2048,128]{2,1,0:T(8,128)(2,1)} all-to-all(bf16[8,2048,128]{2,1,0:T(8,128)(2,1)S(1)} %fusion.7), channel_id=1, replica_groups=mesh['pix'=4,'tm'=8] {'tm'}, dimensions={0} | all-to-all | bytes 8388608 | tf_op jit(solution)/shard_map/all_to_all | solution.py:78
  222.4 6.5 copy.50
  229.8 51.1 %reduce-scatter.2.cloned.1.call-done = bf16[512,1024]{0,1:T(8,128)(2,1)} async-done(((bf16[2048,1024]{0,1:T(8,128)(2,1)}), bf16[512,1024]{0,1:T(8,128)(2,1)}) %reduce-scatter.2.cloned.1.call-update) | async-done | bytes 1048592 | tf_op jit(solution)/shard_map/reduce_scatter | solution.py:81
  283.7 283.2 %while.47 = (s32[]{:T(128)}, bf16[32,16,8,128]{3,2,1,0:T(8,128)(2,1)}, s32[32]{0:T(128)S(1)}, bf16[32,16,18,128]{3,2,1,0:T(8,128)(2,1)S(1)}, bf16[11,128,128]{2,...) while((s32[]{:T(128)}, ...), condition=%wide.region_9.10_spmd, body=%wide.region_6.9_spmd.sunk | while | flops 4210701 | bytes 541657 | solution.py:55
  285.1 17.9 %while.48 = (s32[]{:T(128)}, f32[16,8,128]{2,1,0:T(8,128)S(1)}, s32[]{:T(128)}, s32[]{:T(128)}, bf16[16,18,128]{2,1,0:T(8,128)(2,1)S(1)}, /*index=5*/bf16[11,128...) while((s32[]{:T(128)}, f32[16,8,128]{2,1,0:T(8,128)S(1)}, ...), condition=%wide.region_8.8_spmd, body=%wide.region_7.7_spmd.sunk | while | flops 4210697 | bytes 196808 | solution.py:51
  305.0 17.9 %while.48 = (s32[]{:T(128)}, f32[16,8,128]{2,1,0:T(8,128)S(1)}, s32[]{:T(128)}, s32[]{:T(128)}, bf16[16,18,128]{2,1,0:T(8,128)(2,1)S(1)}, /*index=5*/bf16[11,128...) while((s32[]{:T(128)}, f32[16,8,128]{2,1,0:T(8,128)S(1)}, ...), condition=%wide.region_8.8_spmd, body=%wide.region_7.7_spmd.sunk | while | flops 4210697 | bytes 196808 | solution.py:51
  325.0 17.9 %while.48 = (s32[]{:T(128)}, f32[16,8,128]{2,1,0:T(8,128)S(1)}, s32[]{:T(128)}, s32[]{:T(128)}, bf16[16,18,128]{2,1,0:T(8,128)(2,1)S(1)}, /*index=5*/bf16[11,128...) while((s32[]{:T(128)}, f32[16,8,128]{2,1,0:T(8,128)S(1)}, ...), condition=%wide.region_8.8_spmd, body=%wide.region_7.7_spmd.sunk | while | flops 4210697 | bytes 196808 | solution.py:51
  344.9 17.9 %while.48 = (s32[]{:T(128)}, f32[16,8,128]{2,1,0:T(8,128)S(1)}, s32[]{:T(128)}, s32[]{:T(128)}, bf16[16,18,128]{2,1,0:T(8,128)(2,1)S(1)}, /*index=5*/bf16[11,128...) while((s32[]{:T(128)}, f32[16,8,128]{2,1,0:T(8,128)S(1)}, ...), condition=%wide.region_8.8_spmd, body=%wide.region_7.7_spmd.sunk | while | flops 4210697 | bytes 196808 | solution.py:51
  364.8 17.9 %while.48 = (s32[]{:T(128)}, f32[16,8,128]{2,1,0:T(8,128)S(1)}, s32[]{:T(128)}, s32[]{:T(128)}, bf16[16,18,128]{2,1,0:T(8,128)(2,1)S(1)}, /*index=5*/bf16[11,128...) while((s32[]{:T(128)}, f32[16,8,128]{2,1,0:T(8,128)S(1)}, ...), condition=%wide.region_8.8_spmd, body=%wide.region_7.7_spmd.sunk | while | flops 4210697 | bytes 196808 | solution.py:51
  384.7 8.1 %while.48 = (s32[]{:T(128)}, f32[16,8,128]{2,1,0:T(8,128)S(1)}, s32[]{:T(128)}, s32[]{:T(128)}, bf16[16,18,128]{2,1,0:T(8,128)(2,1)S(1)}, /*index=5*/bf16[11,128...) while((s32[]{:T(128)}, f32[16,8,128]{2,1,0:T(8,128)S(1)}, ...), condition=%wide.region_8.8_spmd, body=%wide.region_7.7_spmd.sunk | while | flops 4210697 | bytes 196808 | solution.py:51
  394.9 8.1 %while.48 = (s32[]{:T(128)}, f32[16,8,128]{2,1,0:T(8,128)S(1)}, s32[]{:T(128)}, s32[]{:T(128)}, bf16[16,18,128]{2,1,0:T(8,128)(2,1)S(1)}, /*index=5*/bf16[11,128...) while((s32[]{:T(128)}, f32[16,8,128]{2,1,0:T(8,128)S(1)}, ...), condition=%wide.region_8.8_spmd, body=%wide.region_7.7_spmd.sunk | while | flops 4210697 | bytes 196808 | solution.py:51
  405.1 8.1 %while.48 = (s32[]{:T(128)}, f32[16,8,128]{2,1,0:T(8,128)S(1)}, s32[]{:T(128)}, s32[]{:T(128)}, bf16[16,18,128]{2,1,0:T(8,128)(2,1)S(1)}, /*index=5*/bf16[11,128...) while((s32[]{:T(128)}, f32[16,8,128]{2,1,0:T(8,128)S(1)}, ...), condition=%wide.region_8.8_spmd, body=%wide.region_7.7_spmd.sunk | while | flops 4210697 | bytes 196808 | solution.py:51
  415.2 8.1 %while.48 = (s32[]{:T(128)}, f32[16,8,128]{2,1,0:T(8,128)S(1)}, s32[]{:T(128)}, s32[]{:T(128)}, bf16[16,18,128]{2,1,0:T(8,128)(2,1)S(1)}, /*index=5*/bf16[11,128...) while((s32[]{:T(128)}, f32[16,8,128]{2,1,0:T(8,128)S(1)}, ...), condition=%wide.region_8.8_spmd, body=%wide.region_7.7_spmd.sunk | while | flops 4210697 | bytes 196808 | solution.py:51
  425.4 8.1 %while.48 = (s32[]{:T(128)}, f32[16,8,128]{2,1,0:T(8,128)S(1)}, s32[]{:T(128)}, s32[]{:T(128)}, bf16[16,18,128]{2,1,0:T(8,128)(2,1)S(1)}, /*index=5*/bf16[11,128...) while((s32[]{:T(128)}, f32[16,8,128]{2,1,0:T(8,128)S(1)}, ...), condition=%wide.region_8.8_spmd, body=%wide.region_7.7_spmd.sunk | while | flops 4210697 | bytes 196808 | solution.py:51
  435.6 8.1 %while.48 = (s32[]{:T(128)}, f32[16,8,128]{2,1,0:T(8,128)S(1)}, s32[]{:T(128)}, s32[]{:T(128)}, bf16[16,18,128]{2,1,0:T(8,128)(2,1)S(1)}, /*index=5*/bf16[11,128...) while((s32[]{:T(128)}, f32[16,8,128]{2,1,0:T(8,128)S(1)}, ...), condition=%wide.region_8.8_spmd, body=%wide.region_7.7_spmd.sunk | while | flops 4210697 | bytes 196808 | solution.py:51
  445.7 8.1 %while.48 = (s32[]{:T(128)}, f32[16,8,128]{2,1,0:T(8,128)S(1)}, s32[]{:T(128)}, s32[]{:T(128)}, bf16[16,18,128]{2,1,0:T(8,128)(2,1)S(1)}, /*index=5*/bf16[11,128...) while((s32[]{:T(128)}, f32[16,8,128]{2,1,0:T(8,128)S(1)}, ...), condition=%wide.region_8.8_spmd, body=%wide.region_7.7_spmd.sunk | while | flops 4210697 | bytes 196808 | solution.py:51
  455.9 8.1 %while.48 = (s32[]{:T(128)}, f32[16,8,128]{2,1,0:T(8,128)S(1)}, s32[]{:T(128)}, s32[]{:T(128)}, bf16[16,18,128]{2,1,0:T(8,128)(2,1)S(1)}, /*index=5*/bf16[11,128...) while((s32[]{:T(128)}, f32[16,8,128]{2,1,0:T(8,128)S(1)}, ...), condition=%wide.region_8.8_spmd, body=%wide.region_7.7_spmd.sunk | while | flops 4210697 | bytes 196808 | solution.py:51
  466.1 4.9 while.48
  473.0 4.9 while.48
  479.9 4.9 while.48
  486.8 4.9 while.48
  493.8 4.9 while.48
  500.7 4.9 while.48
  507.6 4.9 while.48
  514.5 4.9 while.48
  521.4 4.9 while.48
  528.3 4.9 while.48
  566.9 2.5 copy.65
  569.4 55.0 %all-gather.2.cloned.1.call-done = bf16[2048,1024]{1,0:T(8,128)(2,1)} async-done(((bf16[512,1024]{1,0:T(8,128)(2,1)}), bf16[2048,1024]{1,0:T(8,128)(2,1)}) %all-gather.2.cloned.1.call-update) | async-done | bytes 4194320 | tf_op jit(solution)/shard_map/all_gather | solution.py:87
  624.4 6.5 copy.52
  630.9 4.6 all-to-all-start.1
  635.5 4.5 scatter_custom_fusion.1
  641.2 88.4 %all-to-all-done.1 = bf16[2048,8,128]{0,2,1:T(8,128)(2,1)} async-done(((bf16[2048,8,128]{0,2,1:T(8,128)(2,1)}), bf16[2048,8,128]{0,2,1:T(8,128)(2,1)}, u32[]{:S(2)}, u32[]{:S(2)}) %all-to-all-start.1) | async-done | bytes 4194336 | tf_op jit(solution)/shard_map/all_to_all | solution.py:88
  729.6 6.4 copy.53
  736.1 10.6 %gather_fusion.1 = bf16[1024,16,128]{2,1,0:T(8,128)(2,1)} fusion(bf16[1024,16,128]{2,1,0:T(8,128)(2,1)} %bitcast.73, s32[1024]{0:T(1024)S(1)} %fusion.23), kind=kCustom, calls=%fused_computation.1 | custom fusion | bytes 8392704 | tf_op jit(solution)/shard_map/jit(_take)/gather | solution.py:92
  746.6 7.7 bitcast_select_fusion.1
  754.3 8.5 %gather_fusion.2 = bf16[80,512,128]{2,1,0:T(8,128)(2,1)} fusion(bf16[32,512,128]{2,1,0:T(8,128)(2,1)} %bitcast_select_fusion.1, s32[1024]{0:T(1024)S(1)} %pad_clamp_fusion), kind=kCustom, calls=%fused_computation.2 | custom fusion | bytes 20971840 | tf_op jit(solution)/shard_map/jit(_take)/gather | solution.py:100
  762.8 14.6 %copy.58 = bf16[20,4,512,128]{2,3,1,0:T(8,128)(2,1)} copy(bf16[20,4,512,128]{3,2,1,0:T(8,128)(2,1)} %bitcast.66) | data formatting | bytes 20971520 | tf_op jit(solution)/shard_map/jit(_take)/gather | solution.py:100
  777.3 8.8 %fusion.13 = bf16[20,128,128]{1,2,0:T(8,128)(2,1)S(1)} fusion(bf16[20,128,128]{1,2,0:T(8,128)(2,1)S(1)} %copy-done.1, bf16[20,4,128,512]{3,2,1,0:T(8,128)(2,1)} %param.12, bf16[20,4,512,128]{2,3,1,0:T(8,128)(2,1)} %copy.58, pred[20,4]{1,0:T(8,128)(4,1)S(1)} %copy.54), kind=kOutput, calls=%fused_computation.24 | convolution fusion | flops 1348403200 | bytes 22282320 | tf_op jit(solution)/shard_map/nspc,nscf->npf/dot_general | solution.py:101
  787.2 4.2 dynamic-slice_select_fusion
  (320 shorter events, 186.7 us)
Async XLA Ops:
  7.2 273.7 %reduce-scatter.2.cloned.1.call-start = ((), (), s32[]{:S(2)}) async-start(), calls=%async_computation.3 | async-start | bytes 5242880 | tf_op jit(solution)/shard_map/reduce_scatter | solution.py:81
  18.1 14.1 %copy-start = (bf16[20,128,128]{1,2,0:T(8,128)(2,1)}, bf16[20,128,128]{1,2,0:T(8,128)(2,1)S(1)}, u32[]{:S(2)}) copy-start(bf16[20,128,128]{1,2,0:T(8,128)(2,1)S(1)} %copy.48) | copy-start | bytes 1966084
  32.1 21.3 %copy-start.3 = (s32[20,4]{0,1:T(4,128)S(1)}, s32[20,4]{0,1:T(4,128)}, u32[]{:S(2)}) copy-start(s32[20,4]{0,1:T(4,128)} %param.13) | copy-start | bytes 964
  228.9 0.7 copy-start.4
  228.9 395.5 %all-gather.2.cloned.1.call-start = ((), (), s32[]{:S(2)}) async-start(), calls=%async_computation.4 | async-start | bytes 5242880 | tf_op jit(solution)/shard_map/all_gather | solution.py:87
  630.9 98.7 %all-to-all-start.1 = ((bf16[2048,8,128]{0,2,1:T(8,128)(2,1)}), bf16[2048,8,128]{0,2,1:T(8,128)(2,1)}, u32[]{:S(2)}, u32[]{:S(2)}) async-start(bf16[2048,8,128]{0,2,1:T(8,128)(2,1)} %bitcast.69), calls=%async_computation.2 | async-start | bytes 8388608 | tf_op jit(solution)/shard_map/all_to_all | solution.py:88
  640.6 95.5 %copy-start.2 = (pred[16384]{0:T(1024)(128)(4,1)}, pred[16384]{0:T(1024)(128)(4,1)S(1)}, u32[]{:S(2)}) copy-start(pred[16384]{0:T(1024)(128)(4,1)S(1)} %broadcast_in_dim.94) | copy-start | bytes 49156
  762.8 14.6 %copy-start.1 = (bf16[20,128,128]{1,2,0:T(8,128)(2,1)S(1)}, bf16[20,128,128]{1,2,0:T(8,128)(2,1)}, u32[]{:S(2)}) copy-start(bf16[20,128,128]{1,2,0:T(8,128)(2,1)} %copy-done) | copy-start | bytes 1966084
  777.3 9.9 %dynamic-slice-start = ((pred[16384]{0:T(1024)(128)(4,1)}, s32[]{:T(128)}), pred[4096]{0:T(1024)(128)(4,1)S(1)}, s32[]{:S(2)}) async-start(pred[16384]{0:T(1024)(128)(4,1)} %copy-done.2, s32[]{:T(128)} %select_n.146), calls=%async_computation.5 | async-start | bytes 8704 | tf_op jit(solution)/shard_map/dynamic_slice | solution.py:96
Sparse Core Ops, SparseCore 0:
  229.1 51.7 reduce-scatter.1
  569.5 54.8 all-gather.1
where the time goes:
time: 815 us; the launch traced here: 798 us
  waiting for transfers between devices  195 us (24%)
  local copies, waits for them, and re-layouts  152 us (19%)
  matrix products  144 us (18%)
  loops' own time  120 us (15%)
  blocking collectives  100 us (12%)
  other arithmetic  69 us (8%)
  between operations  14.2 us (2%)
    dot_general x134, matrix products, one_offset(): jnp.einsum('gbf,fh->gbh', shifted, matrix, preferred_element_type=jnp.flo...  121 us
    all_to_all x1, blocking collectives, shards(): lax.all_to_all(partial_value.astype(jnp.bfloat16), 'tm', split_axis=0, co...  100 us
    another operation x32, loops' own time, one_group(): result = lax.fori_loop(0, 2 * band_reach + 1, one_offset, zero_block)  96.8 us
    all_to_all x1, waiting for transfers between devices, shards(): lax.all_to_all(collected, 'tm', split_axis=1, concat_axis=0, tiled=True)  88.4 us
    all_gather x1, waiting for transfers between devices, shards(): collected = lax.all_gather(traces_here, 'pix', axis=0, tiled=True)  55 us
    reduce_scatter x1, waiting for transfers between devices, shards(): lax.psum_scatter(moved.astype(jnp.float32).astype(jnp.bfloat16), 'pix', s...  51.1 us
    scatter-add x1, other arithmetic, shards(): partial_value = blank_sum.at[block_ids.reshape(-1)].add(contrib.reshape(-...  45.8 us
    another operation x1, loops' own time, band_filter(): filtered = lax.fori_loop(0, local_groups, one_group, blank_out)  23.1 us
  transfers between devices with their start and end apart: 3, of which 3 were waited for; matrix products, arithmetic and copies ran while one was open for 1% of the time, Pallas kernels for 0%

commit v1 on v0

v1 whole, which is shorter than its diff:
```python
import functools

import jax
import jax.numpy as jnp
from jax import lax
from jax.experimental import pallas as pl
from jax.experimental.pallas import tpu as pltpu
from jax.sharding import PartitionSpec as P

K = 16384
CBLK = 512
GROUP = 16
BMAX = 5
FR = 128
LANE = 128
MESH = pl.DeviceIdType.MESH
VMEM_LIMIT = 56 * 1024 * 1024


def project_kernel(ids_ref, movie_ref, noise_ref, feet_ref, out_ref, acc_ref):
    tile = pl.program_id(0)

    @pl.when(tile == 0)
    def _():
        acc_ref[...] = jnp.zeros_like(acc_ref)

    pixels = movie_ref[0].astype(jnp.float32)
    weight = noise_ref[pl.ds(tile, 1), :]
    weighted = (pixels.T * weight).astype(jnp.bfloat16)
    slots = feet_ref.shape[1]
    for slot in range(slots):
        block = ids_ref[tile * slots + slot]
        acc_ref[block] += jnp.dot(
            weighted, feet_ref[0, slot], preferred_element_type=jnp.float32
        )

    @pl.when(tile == pl.num_programs(0) - 1)
    def _():
        def put(b, carry):
            out_ref[b] = acc_ref[b].astype(out_ref.dtype)
            return carry

        lax.fori_loop(0, out_ref.shape[0], put, 0)


def project(movie, noise_weight, footprints, block_ids):
    tiles, slots, pixels, width = footprints.shape
    frames = movie.shape[2]
    blocks = K // CBLK
    return pl.pallas_call(
        project_kernel,
        grid_spec=pltpu.PrefetchScalarGridSpec(
            num_scalar_prefetch=1,
            grid=(tiles,),
            in_specs=[
                pl.BlockSpec((1, pixels, frames), lambda n, ids: (n, 0, 0)),
                pl.BlockSpec((tiles, pixels), lambda n, ids: (0, 0)),
                pl.BlockSpec((1, slots, pixels, width), lambda n, ids: (n, 0, 0, 0)),
            ],
            out_specs=pl.BlockSpec((blocks, frames, width), lambda n, ids: (0, 0, 0)),
            scratch_shapes=[pltpu.VMEM((blocks, frames, width), jnp.float32)],
        ),
        out_shape=jax.ShapeDtypeStruct((blocks, frames, width), jnp.bfloat16),
        compiler_params=pltpu.CompilerParams(vmem_limit_bytes=VMEM_LIMIT),
        name="project",
    )(block_ids.reshape(-1), movie, noise_weight, footprints)


def rebuild_kernel(ids_ref, movie_ref, feet_ref, traces_ref, out_ref):
    tile = pl.program_id(0)
    slots = feet_ref.shape[1]
    total = movie_ref[0].astype(jnp.float32)
    for slot in range(slots):
        block = ids_ref[tile * slots + slot]
        total = total - jnp.dot(
            feet_ref[0, slot], traces_ref[block], preferred_element_type=jnp.float32
        )
    out_ref[0] = total.astype(out_ref.dtype)


def rebuild(movie, footprints, block_ids, traces):
    tiles, slots, pixels, width = footprints.shape
    frames = movie.shape[2]
    blocks = K // CBLK
    return pl.pallas_call(
        rebuild_kernel,
        grid_spec=pltpu.PrefetchScalarGridSpec(
            num_scalar_prefetch=1,
            grid=(tiles,),
            in_specs=[
                pl.BlockSpec((1, pixels, frames), lambda n, ids: (n, 0, 0)),
                pl.BlockSpec((1, slots, pixels, width), lambda n, ids: (n, 0, 0, 0)),
                pl.BlockSpec((blocks, width, frames), lambda n, ids: (0, 0, 0)),
            ],
            out_specs=pl.BlockSpec((1, pixels, frames), lambda n, ids: (n, 0, 0)),
        ),
        out_shape=jax.ShapeDtypeStruct(movie.shape, jnp.bfloat16),
        compiler_params=pltpu.CompilerParams(vmem_limit_bytes=VMEM_LIMIT),
        name="rebuild",
    )(block_ids.reshape(-1), movie, footprints, traces.reshape(blocks, width, frames))


def middle_kernel(
    n_pix, n_tm, part_ref, reach_ref, prec_ref, out_ref,
    rs_buf, x_buf, xt_buf, y_buf,
    rs_s, rs_r, a_s, a_r, b_s, b_r, g_s, g_r,
):
    chunks = rs_buf.shape[0]
    blocks_chunk = rs_buf.shape[2]
    lanes = xt_buf.shape[3]
    groups = CBLK // lanes
    blocks_pix = chunks * blocks_chunk
    me_p = lax.axis_index("pix")
    me_t = lax.axis_index("tm")

    def pix_at(e):
        return lax.rem(me_p + e, n_pix)

    def tm_at(e):
        return lax.rem(me_t + e, n_tm)

    barrier = pltpu.get_barrier_semaphore()
    for e in range(1, n_pix):
        pl.semaphore_signal(
            barrier, inc=1, device_id={"pix": pix_at(e)}, device_id_type=MESH
        )
    for e in range(1, n_tm):
        pl.semaphore_signal(
            barrier, inc=1, device_id={"tm": tm_at(e)}, device_id_type=MESH
        )
    pl.semaphore_wait(barrier, n_pix + n_tm - 2)

    def rs_copy(c, e):
        peer = pix_at(e)
        return pltpu.make_async_remote_copy(
            src_ref=part_ref.at[pl.ds(peer * blocks_pix + c * blocks_chunk, blocks_chunk)],
            dst_ref=rs_buf.at[c, e - 1],
            send_sem=rs_s.at[c, e - 1],
            recv_sem=rs_r.at[c, e - 1],
            device_id={"pix": peer},
            device_id_type=MESH,
        )

    def a_copy(c, e):
        peer = tm_at(e)
        return pltpu.make_async_remote_copy(
            src_ref=x_buf.at[c, peer],
            dst_ref=xt_buf.at[c, me_t + BMAX],
            send_sem=a_s.at[c, e - 1],
            recv_sem=a_r.at[c, e - 1],
            device_id={"tm": peer},
            device_id_type=MESH,
        )

    def b_copy(c, e):
        peer = tm_at(e)
        return pltpu.make_async_remote_copy(
            src_ref=y_buf.at[c, peer],
            dst_ref=out_ref.at[me_p, c, me_t],
            send_sem=b_s.at[c, e - 1],
            recv_sem=b_r.at[c, e - 1],
            device_id={"tm": peer},
            device_id_type=MESH,
        )

    def g_copy(c, e):
        peer = pix_at(e)
        return pltpu.make_async_remote_copy(
            src_ref=out_ref.at[me_p, c],
            dst_ref=out_ref.at[me_p, c],
            send_sem=g_s.at[c, e - 1],
            recv_sem=g_r.at[c, e - 1],
            device_id={"pix": peer},
            device_id_type=MESH,
        )

    for c in range(chunks):
        for e in range(1, n_pix):
            rs_copy(c, e).start()

    edge = jnp.zeros((BMAX,) + xt_buf.shape[2:], xt_buf.dtype)
    for c in range(chunks):
        xt_buf[c, pl.ds(0, BMAX)] = edge
        xt_buf[c, pl.ds(BMAX + n_tm, BMAX)] = edge

    def sum_chunk(c):
        for e in range(1, n_pix):
            rs_copy(c, e).wait_recv()
        for part in range(n_tm):
            b, g = part // groups, part % groups
            span = slice(g * lanes, (g + 1) * lanes)
            total = part_ref[me_p * blocks_pix + c * blocks_chunk + b, :, span].astype(jnp.float32)
            for e in range(1, n_pix):
                total = total + rs_buf[c, e - 1, b, :, span].astype(jnp.float32)
            x_buf[c, part] = total.astype(x_buf.dtype)
        for e in range(1, n_tm):
            a_copy(c, e).start()
        xt_buf[c, me_t + BMAX] = x_buf[c, me_t]

    def filter_chunk(c):
        for e in range(1, n_tm):
            a_copy(c, e).wait_recv()
        reach = reach_ref[pl.ds(c, 1), :]
        keep = [
            jnp.where(reach >= k, 1.0, 0.0).astype(jnp.bfloat16) for k in range(BMAX + 1)
        ]

        def one_block(i):
            source = jnp.concatenate(
                [xt_buf[c, i + d + BMAX] * keep[abs(d)] for d in range(-BMAX, BMAX + 1)],
                axis=0,
            )
            result = jnp.dot(prec_ref[...], source, preferred_element_type=jnp.float32)
            return result.T.astype(jnp.bfloat16)

        def step(e, carry):
            peer = tm_at(e)
            y_buf[c, peer] = one_block(peer)
            return carry

        lax.fori_loop(0, n_tm, step, 0)
        for e in range(1, n_tm):
            b_copy(c, e).start()
        out_ref[me_p, c, me_t] = y_buf[c, me_t]

    def gather_chunk(c):
        for e in range(1, n_tm):
            b_copy(c, e).wait_recv()
        for e in range(1, n_pix):
            g_copy(c, e).start()

    for t in range(chunks + 2):
        if t < chunks:
            sum_chunk(t)
        if 0 <= t - 1 < chunks:
            filter_chunk(t - 1)
        if 0 <= t - 2:
            gather_chunk(t - 2)

    for c in range(chunks):
        for e in range(1, n_pix):
            g_copy(c, e).wait_recv()
    for c in range(chunks):
        for e in range(1, n_pix):
            rs_copy(c, e).wait_send()
            g_copy(c, e).wait_send()
        for e in range(1, n_tm):
            a_copy(c, e).wait_send()
            b_copy(c, e).wait_send()


def middle(partial_value, band_width, precision_blocks):
    blocks, frames, width = partial_value.shape
    n_pix, n_tm = lax.axis_size("pix"), lax.axis_size("tm")
    chunks = K // (n_pix * n_tm * LANE)
    blocks_chunk = blocks // (n_pix * chunks)
    reach = jnp.repeat(band_width, GROUP).reshape(n_pix, chunks, n_tm, LANE)
    reach = lax.dynamic_index_in_dim(reach, lax.axis_index("pix"), 0, keepdims=False)
    reach = lax.dynamic_index_in_dim(reach, lax.axis_index("tm"), 1, keepdims=False)
    stacked = precision_blocks.reshape(-1, FR).T
    dma = pltpu.SemaphoreType.DMA
    bf16 = jnp.bfloat16
    vmem = pl.BlockSpec(memory_space=pltpu.VMEM)
    gathered = pl.pallas_call(
        functools.partial(middle_kernel, n_pix, n_tm),
        out_shape=jax.ShapeDtypeStruct((n_pix, chunks, n_tm, LANE, frames), bf16),
        in_specs=[vmem, vmem, vmem],
        out_specs=vmem,
        scratch_shapes=[
            pltpu.VMEM((chunks, n_pix - 1, blocks_chunk, frames, width), bf16),
            pltpu.VMEM((chunks, n_tm, frames, LANE), bf16),
            pltpu.VMEM((chunks, n_tm + 2 * BMAX, frames, LANE), bf16),
            pltpu.VMEM((chunks, n_tm, LANE, frames), bf16),
            dma((chunks, n_pix - 1)), dma((chunks, n_pix - 1)),
            dma((chunks, n_tm - 1)), dma((chunks, n_tm - 1)),
            dma((chunks, n_tm - 1)), dma((chunks, n_tm - 1)),
            dma((chunks, n_pix - 1)), dma((chunks, n_pix - 1)),
        ],
        compiler_params=pltpu.CompilerParams(
            collective_id=0, has_side_effects=True, vmem_limit_bytes=VMEM_LIMIT
        ),
        name="middle",
    )(partial_value, reach, stacked)
    traces = lax.dynamic_index_in_dim(gathered, lax.axis_index("pix"), 0, keepdims=False)
    return gathered.reshape(K, frames), traces.reshape(K // n_pix, frames)


def middle_plain(partial_value, band_width, precision_blocks):
    blocks, frames, width = partial_value.shape
    n_pix, n_tm = lax.axis_size("pix"), lax.axis_size("tm")
    summed = lax.psum_scatter(partial_value, "pix", scatter_dimension=0, tiled=True)
    rows = summed.transpose(0, 2, 1).reshape(K // n_pix, frames)
    moved = lax.all_to_all(rows, "tm", split_axis=0, concat_axis=1, tiled=True)
    here = moved.shape[0]
    start = (lax.axis_index("pix") * n_tm + lax.axis_index("tm")) * here
    widths = lax.dynamic_slice_in_dim(jnp.repeat(band_width, GROUP), start, here)
    nblocks = moved.shape[1] // FR
    padded = jnp.pad(moved.reshape(here, nblocks, FR), ((0, 0), (BMAX, BMAX), (0, 0)))
    filtered = jnp.zeros((here, nblocks, FR), jnp.float32)
    for d in range(2 * BMAX + 1):
        term = jnp.einsum(
            "kbf,fh->kbh", padded[:, d:d + nblocks], precision_blocks[d],
            preferred_element_type=jnp.float32,
        )
        filtered = filtered + jnp.where((abs(d - BMAX) <= widths)[:, None, None], term, 0.0)
    local = filtered.reshape(here, nblocks * FR).astype(jnp.bfloat16)
    traces = lax.all_to_all(local, "tm", split_axis=1, concat_axis=0, tiled=True)
    return lax.all_gather(traces, "pix", axis=0, tiled=True), traces


def shards(movie, noise_weight, footprints, block_ids, band_width, precision_blocks):
    n_pix, n_tm = lax.axis_size("pix"), lax.axis_size("tm")
    partial_value = project(movie, noise_weight, footprints, block_ids)
    fits = movie.shape[2] == FR and K % (n_pix * n_tm * LANE) == 0
    fits = fits and (K // CBLK) % (n_pix * (K // (n_pix * n_tm * LANE))) == 0
    form = middle if fits else middle_plain
    all_traces, traces = form(partial_value, band_width, precision_blocks)
    residual = rebuild(movie, footprints, block_ids, all_traces)
    return (traces, residual)


def solution(mesh):
    return jax.shard_map(
        shards,
        mesh=mesh,
        in_specs=(
            P("pix", None, "tm"),
            P("pix", None),
            P("pix", None, None, None),
            P("pix", None),
            P(),
            P(),
        ),
        out_specs=(P("pix", "tm"), P("pix", None, "tm")),
        check_vma=False,
    )
```

time: 815 us -> 148 us (0.18); the launches traced: 798 us -> 147 us
  waiting for transfers between devices: 195 us -> 0 us
  local copies, waits for them, and re-layouts: 152 us -> 7.32 us
  matrix products: 144 us -> 0 us
  Pallas kernels: 0 us -> 139 us
  loops' own time: 120 us -> 0 us
  blocking collectives: 100 us -> 0 us
  other arithmetic: 69 us -> 0 us
  between operations: 14.2 us -> 0.68 us
    dot_general x136 -> x0, matrix products: 144 us -> none  [the longest x134 121 us: one_offset(): jnp.einsum('gbf,fh->gbh', shifted, matrix, preferred_element_type=jnp.flo...]
    pallas_call x0 -> x3, Pallas kernels: none -> 139 us  [the longest x1 104 us: middle(): pl.pallas_call(functools.partial(middle_kernel, n_pix, n_tm), out_shape=j...]
    another operation x33 -> x0, loops' own time: 120 us -> none  [the longest x32 96.8 us: one_group(): result = lax.fori_loop(0, 2 * band_reach + 1, one_offset, zero_block)]
    all_to_all x1 -> x0, blocking collectives: 100 us -> none  [shards(): lax.all_to_all(partial_value.astype(jnp.bfloat16), 'tm', split_axis=0, co...]
    all_to_all x1 -> x0, waiting for transfers between devices: 88.4 us -> none  [shards(): lax.all_to_all(collected, 'tm', split_axis=1, concat_axis=0, tiled=True)]
    all_gather x1 -> x0, waiting for transfers between devices: 55 us -> none  [shards(): collected = lax.all_gather(traces_here, 'pix', axis=0, tiled=True)]
    reduce_scatter x1 -> x0, waiting for transfers between devices: 51.1 us -> none  [shards(): lax.psum_scatter(moved.astype(jnp.float32).astype(jnp.bfloat16), 'pix', s...]
    scatter-add x1 -> x0, other arithmetic: 45.8 us -> none  [shards(): partial_value = blank_sum.at[block_ids.reshape(-1)].add(contrib.reshape(-...]
  transfers between devices with their start and end apart: 3 -> 0, of which waited for: 3 -> 0; matrix products, arithmetic and copies ran while one was open for 1% -> 0% of each run, Pallas kernels for 0% -> 0%
where the time goes in v1:
time: 148 us; the launch traced here: 147 us
  Pallas kernels  139 us (94%)
  local copies, waits for them, and re-layouts  7.32 us (5%)
    pallas_call x1, Pallas kernels, middle(): pl.pallas_call(functools.partial(middle_kernel, n_pix, n_tm), out_shape=j...  104 us
    pallas_call x1, Pallas kernels, project(): pl.pallas_call(project_kernel, grid_spec=pltpu.PrefetchScalarGridSpec(num...  18.5 us
    pallas_call x1, Pallas kernels, rebuild(): pl.pallas_call(rebuild_kernel, grid_spec=pltpu.PrefetchScalarGridSpec(num...  17.3 us

profile of v1, /device:TPU:0, one launch (start us, length us, event | category | flops | bytes accessed | tf_op | source)
XLA Modules:
  0.0 147.4 jit_solution(2677976652658940316)
XLA Ops:
  0.6 0.8 copy.10
  1.4 0.6 reshape.19.ids_ref
  2.0 0.8 broadcast_in_dim.7
  2.8 1.9 %copy.12 = bf16[1408,128]{0,1:T(8,128)(2,1)} copy(bf16[1408,128]{1,0:T(8,128)(2,1)} %bitcast.13) | data formatting | bytes 720896 | tf_op jit(solution)/shard_map/reshape | solution.py:260
  4.7 0.2 broadcast_in_dim.8
  4.9 0.2 broadcast_in_dim.9
  5.1 0.6 dynamic-slice_bitcast_fusion.reach_ref
  5.7 18.5 %project.1.part_ref = bf16[32,128,512]{2,1,0:T(8,128)(2,1)} custom-call(s32[80]{0:T(128)} %reshape.19.ids_ref, bf16[20,128,128]{2,1,0:T(8,128)(2,1)} %movie_ref.3, f32[20,128]{1,0:T(8,128)} %noise_ref.1, bf16[20,4,128,512]{3,2,1,0:T(8,128)(2,1)} %feet_ref.3), custom_call_target="tpu_custom_call" | custom-call | tf_op jit(solution)/shard_map/project/pallas_call | solution.py:50
  24.2 103.5 %middle.1 = bf16[4,4,8,128,128]{4,3,2,1,0:T(8,128)(2,1)} custom-call(bf16[32,128,512]{2,1,0:T(8,128)(2,1)} %project.1.part_ref, s32[4,128]{1,0:T(4,128)} %dynamic-slice_bitcast_fusion.reach_ref, bf16[128,1408]{1,0:T(8,128)(2,1)} %bitcast.11), custom_call_target="tpu_custom_call" | custom-call | tf_op jit(solution)/shard_map/middle/pallas_call | solution.py:264
  127.7 17.3 %rebuild.1 = bf16[20,128,128]{2,1,0:T(8,128)(2,1)} custom-call(s32[80]{0:T(128)} %reshape.19.ids_ref, bf16[20,128,128]{2,1,0:T(8,128)(2,1)} %movie_ref.3, bf16[20,4,128,512]{3,2,1,0:T(8,128)(2,1)} %feet_ref.3, bf16[32,512,128]{2,1,0:T(8,128)(2,1)} %bitcast.10), custom_call_target="tpu_custom_call" | custom-call | tf_op jit(solution)/shard_map/rebuild/pallas_call | solution.py:85
  145.1 2.3 %constant_dynamic-slice_fusion = bf16[1,4,8,128,128]{4,3,2,1,0:T(8,128)(2,1)} fusion(bf16[4,4,8,128,128]{4,3,2,1,0:T(8,128)(2,1)} %middle.1, s32[]{:T(128)S(6)} %select_n.14), kind=kLoop, calls=%fused_computation.1 | loop fusion | bytes 2097156 | tf_op jit(solution)/shard_map/jit(dynamic_index_in_dim)/dynamic_slice | solution.py:284
  (1 shorter events, 0.0 us)

commit v2 on v1

v2 whole, which is shorter than its diff:
```python
import functools

import jax
import jax.numpy as jnp
from jax import lax
from jax.experimental import pallas as pl
from jax.experimental.pallas import tpu as pltpu
from jax.sharding import PartitionSpec as P

K = 16384
CBLK = 512
GROUP = 16
BMAX = 5
FR = 128
LANE = 128
SIDE = 2
HALVES = 2
MESH = pl.DeviceIdType.MESH
VMEM_LIMIT = 56 * 1024 * 1024


def tile_batch(tiles):
    return 4 if tiles % 4 == 0 else 1


def project_kernel(ids_ref, movie_ref, noise_ref, feet_ref, out_ref, acc_ref):
    tile = pl.program_id(0)

    @pl.when(tile == 0)
    def _():
        acc_ref[...] = jnp.zeros_like(acc_ref)

    batch, slots = feet_ref.shape[:2]
    for member in range(batch):
        at = tile * batch + member
        pixels = movie_ref[member].astype(jnp.float32)
        weighted = (pixels.T * noise_ref[pl.ds(at, 1), :]).astype(jnp.bfloat16)
        products = [
            jnp.dot(weighted, feet_ref[member, slot], preferred_element_type=jnp.float32)
            for slot in range(slots)
        ]
        for slot in range(slots):
            acc_ref[ids_ref[at * slots + slot]] += products[slot]

    @pl.when(tile == pl.num_programs(0) - 1)
    def _():
        def put(b, carry):
            out_ref[b] = acc_ref[b].astype(out_ref.dtype)
            return carry

        lax.fori_loop(0, out_ref.shape[0], put, 0)


def project(movie, noise_weight, footprints, block_ids):
    tiles, slots, pixels, width = footprints.shape
    frames = movie.shape[2]
    blocks = K // CBLK
    batch = tile_batch(tiles)
    return pl.pallas_call(
        project_kernel,
        grid_spec=pltpu.PrefetchScalarGridSpec(
            num_scalar_prefetch=1,
            grid=(tiles // batch,),
            in_specs=[
                pl.BlockSpec((batch, pixels, frames), lambda n, ids: (n, 0, 0)),
                pl.BlockSpec((tiles, pixels), lambda n, ids: (0, 0)),
                pl.BlockSpec((batch, slots, pixels, width), lambda n, ids: (n, 0, 0, 0)),
            ],
            out_specs=pl.BlockSpec((blocks, frames, width), lambda n, ids: (0, 0, 0)),
            scratch_shapes=[pltpu.VMEM((blocks, frames, width), jnp.float32)],
        ),
        out_shape=jax.ShapeDtypeStruct((blocks, frames, width), jnp.bfloat16),
        compiler_params=pltpu.CompilerParams(vmem_limit_bytes=VMEM_LIMIT),
        name="project",
    )(block_ids.reshape(-1), movie, noise_weight, footprints)


def rebuild_kernel(ids_ref, me_ref, movie_ref, feet_ref, traces_ref, own_ref, out_ref):
    tile = pl.program_id(0)

    @pl.when(tile == 0)
    def _():
        count = own_ref.shape[0]

        def put(b, carry):
            own_ref[b] = traces_ref[me_ref[0] * count + b]
            return carry

        lax.fori_loop(0, count, put, 0)

    batch, slots = feet_ref.shape[:2]
    for member in range(batch):
        at = tile * batch + member
        rebuilt = None
        for slot in range(slots):
            term = jnp.dot(
                feet_ref[member, slot], traces_ref[ids_ref[at * slots + slot]],
                preferred_element_type=jnp.float32,
            )
            rebuilt = term if rebuilt is None else rebuilt + term
        out_ref[member] = (movie_ref[member].astype(jnp.float32) - rebuilt).astype(out_ref.dtype)


def rebuild(movie, footprints, block_ids, traces):
    tiles, slots, pixels, width = footprints.shape
    frames = movie.shape[2]
    blocks = K // CBLK
    n_pix = lax.axis_size("pix")
    batch = tile_batch(tiles)
    own = (blocks // n_pix, width, frames)
    own_traces, residual = pl.pallas_call(
        rebuild_kernel,
        grid_spec=pltpu.PrefetchScalarGridSpec(
            num_scalar_prefetch=2,
            grid=(tiles // batch,),
            in_specs=[
                pl.BlockSpec((batch, pixels, frames), lambda n, ids, me: (n, 0, 0)),
                pl.BlockSpec((batch, slots, pixels, width), lambda n, ids, me: (n, 0, 0, 0)),
                pl.BlockSpec((blocks, width, frames), lambda n, ids, me: (0, 0, 0)),
            ],
            out_specs=[
                pl.BlockSpec(own, lambda n, ids, me: (0, 0, 0)),
                pl.BlockSpec((batch, pixels, frames), lambda n, ids, me: (n, 0, 0)),
            ],
        ),
        out_shape=[
            jax.ShapeDtypeStruct(own, jnp.bfloat16),
            jax.ShapeDtypeStruct(movie.shape, jnp.bfloat16),
        ],
        compiler_params=pltpu.CompilerParams(vmem_limit_bytes=VMEM_LIMIT),
        name="rebuild",
    )(
        block_ids.reshape(-1), lax.axis_index("pix").reshape(1),
        movie, footprints, traces.reshape(blocks, width, frames),
    )
    return own_traces.reshape(K // n_pix, frames), residual


def middle_kernel(
    n_pix, n_tm, part_ref, reach_ref, prec_ref, out_ref,
    far_buf, near_buf, hop_out, hop_in, x_buf, xt_buf, y_buf,
    far_s, far_r, near_s, near_r, hop_s, hop_r,
    a_s, a_r, b_s, b_r, g_s, g_r, relay_s, relay_r,
):
    chunks = far_buf.shape[0]
    lanes = xt_buf.shape[3]
    groups = CBLK // lanes
    parts_half = n_tm // HALVES
    me_p = lax.axis_index("pix")
    me_t = lax.axis_index("tm")
    me_x = lax.rem(me_p, SIDE)
    along_x = me_p + 1 - 2 * me_x
    along_y = lax.rem(me_p + SIDE, n_pix)
    across = lax.rem(along_x + SIDE, n_pix)
    first = (along_x, along_y)
    second = (along_y, along_x)

    def tm_at(e):
        return lax.rem(me_t + e, n_tm)

    def part_at(owner, c, h):
        return (owner * chunks + c) * HALVES + h

    barrier = pltpu.get_barrier_semaphore()
    for peer in first:
        pl.semaphore_signal(barrier, inc=1, device_id={"pix": peer}, device_id_type=MESH)
    for e in range(1, n_tm):
        pl.semaphore_signal(
            barrier, inc=1, device_id={"tm": tm_at(e)}, device_id_type=MESH
        )
    pl.semaphore_wait(barrier, len(first) + n_tm - 1)

    def pix_copy(source, target, send, recv, c, h, peer):
        return pltpu.make_async_remote_copy(
            src_ref=source, dst_ref=target, send_sem=send.at[c, h], recv_sem=recv.at[c, h],
            device_id={"pix": peer}, device_id_type=MESH,
        )

    def far_copy(c, h):
        source = part_ref.at[part_at(across, c, h)]
        return pix_copy(source, far_buf.at[c, h], far_s, far_r, c, h, first[h])

    def near_copy(c, h):
        source = part_ref.at[part_at(first[h], c, h)]
        return pix_copy(source, near_buf.at[c, h], near_s, near_r, c, h, first[h])

    def hop_copy(c, h):
        return pix_copy(hop_out.at[c, h], hop_in.at[c, h], hop_s, hop_r, c, h, second[h])

    def g_copy(c, h):
        rows = out_ref.at[me_p, c]
        return pix_copy(rows, rows, g_s, g_r, c, h, first[h])

    def relay_copy(c, h):
        rows = out_ref.at[first[h], c, pl.ds(h * parts_half, parts_half)]
        return pix_copy(rows, rows, relay_s, relay_r, c, h, second[h])

    def a_copy(c, e):
        peer = tm_at(e)
        return pltpu.make_async_remote_copy(
            src_ref=x_buf.at[c, peer],
            dst_ref=xt_buf.at[c, me_t + BMAX],
            send_sem=a_s.at[c, e - 1],
            recv_sem=a_r.at[c, e - 1],
            device_id={"tm": peer},
            device_id_type=MESH,
        )

    def b_copy(c, e):
        peer = tm_at(e)
        return pltpu.make_async_remote_copy(
            src_ref=y_buf.at[c, peer],
            dst_ref=out_ref.at[me_p, c, me_t],
            send_sem=b_s.at[c, e - 1],
            recv_sem=b_r.at[c, e - 1],
            device_id={"tm": peer},
            device_id_type=MESH,
        )

    def send_far(c):
        for h in range(HALVES):
            far_copy(c, h).start()

    def send_near(c):
        for h in range(HALVES):
            near_copy(c, h).start()

    def send_hop(c):
        for h in range(HALVES):
            far_copy(c, h).wait_recv()
            total = part_ref[part_at(second[h], c, h)].astype(jnp.float32)
            total = total + far_buf[c, h].astype(jnp.float32)
            hop_out[c, h] = total.astype(hop_out.dtype)
            hop_copy(c, h).start()

    def sum_chunk(c):
        for h in range(HALVES):
            near_copy(c, h).wait_recv()
            hop_copy(c, h).wait_recv()
            for g in range(groups):
                span = slice(g * lanes, (g + 1) * lanes)
                total = part_ref[part_at(me_p, c, h), :, span].astype(jnp.float32)
                total = total + near_buf[c, h, :, span].astype(jnp.float32)
                total = total + hop_in[c, h, :, span].astype(jnp.float32)
                x_buf[c, h * groups + g] = total.astype(x_buf.dtype)
        for e in range(1, n_tm):
            a_copy(c, e).start()
        xt_buf[c, me_t + BMAX] = x_buf[c, me_t]

    def filter_chunk(c):
        for e in range(1, n_tm):
            a_copy(c, e).wait_recv()
        reach = reach_ref[pl.ds(c, 1), :]
        keep = [
            jnp.where(reach >= k, 1.0, 0.0).astype(jnp.bfloat16) for k in range(BMAX + 1)
        ]

        def one_block(i):
            source = jnp.concatenate(
                [xt_buf[c, i + d + BMAX] * keep[abs(d)] for d in range(-BMAX, BMAX + 1)],
                axis=0,
            )
            result = jnp.dot(prec_ref[...], source, preferred_element_type=jnp.float32)
            return result.T.astype(jnp.bfloat16)

        def step(e, carry):
            peer = tm_at(e)
            y_buf[c, peer] = one_block(peer)
            return carry

        lax.fori_loop(0, n_tm, step, 0)
        for e in range(1, n_tm):
            b_copy(c, e).start()
        out_ref[me_p, c, me_t] = y_buf[c, me_t]

    def gather_chunk(c):
        for e in range(1, n_tm):
            b_copy(c, e).wait_recv()
        for h in range(HALVES):
            g_copy(c, h).start()

    def relay_chunk(c):
        for h in range(HALVES):
            g_copy(c, h).wait_recv()
            relay_copy(c, h).start()

    send_far(0)
    send_near(0)
    edge = jnp.zeros((BMAX,) + xt_buf.shape[2:], xt_buf.dtype)
    for c in range(chunks):
        xt_buf[c, pl.ds(0, BMAX)] = edge
        xt_buf[c, pl.ds(BMAX + n_tm, BMAX)] = edge
    if chunks > 1:
        send_far(1)
    for t in range(chunks + 3):
        if t < chunks:
            send_hop(t)
        if t + 1 < chunks:
            send_near(t + 1)
        if t + 2 < chunks:
            send_far(t + 2)
        if t < chunks:
            sum_chunk(t)
        if 0 <= t - 1 < chunks:
            filter_chunk(t - 1)
        if 0 <= t - 2 < chunks:
            gather_chunk(t - 2)
        if 0 <= t - 3:
            relay_chunk(t - 3)

    for c in range(chunks):
        for h in range(HALVES):
            relay_copy(c, h).wait_recv()
    for c in range(chunks):
        for h in range(HALVES):
            for copy in (far_copy, near_copy, hop_copy, g_copy, relay_copy):
                copy(c, h).wait_send()
        for e in range(1, n_tm):
            a_copy(c, e).wait_send()
            b_copy(c, e).wait_send()


def middle(partial_value, band_width, precision_blocks):
    blocks, frames, width = partial_value.shape
    n_pix, n_tm = lax.axis_size("pix"), lax.axis_size("tm")
    chunks = K // (n_pix * n_tm * LANE)
    reach = jnp.repeat(band_width, GROUP).reshape(n_pix, chunks, n_tm, LANE)
    reach = lax.dynamic_index_in_dim(reach, lax.axis_index("pix"), 0, keepdims=False)
    reach = lax.dynamic_index_in_dim(reach, lax.axis_index("tm"), 1, keepdims=False)
    stacked = precision_blocks.reshape(-1, FR).T
    dma = pltpu.SemaphoreType.DMA
    bf16 = jnp.bfloat16
    vmem = pl.BlockSpec(memory_space=pltpu.VMEM)
    gathered = pl.pallas_call(
        functools.partial(middle_kernel, n_pix, n_tm),
        out_shape=jax.ShapeDtypeStruct((n_pix, chunks, n_tm, LANE, frames), bf16),
        in_specs=[vmem, vmem, vmem],
        out_specs=vmem,
        scratch_shapes=[pltpu.VMEM((chunks, HALVES, frames, width), bf16)] * 4 + [
            pltpu.VMEM((chunks, n_tm, frames, LANE), bf16),
            pltpu.VMEM((chunks, n_tm + 2 * BMAX, frames, LANE), bf16),
            pltpu.VMEM((chunks, n_tm, LANE, frames), bf16),
        ] + [dma((chunks, HALVES))] * 6 + [dma((chunks, n_tm - 1))] * 4
        + [dma((chunks, HALVES))] * 4,
        compiler_params=pltpu.CompilerParams(
            collective_id=0, has_side_effects=True, vmem_limit_bytes=VMEM_LIMIT
        ),
        name="middle",
    )(partial_value, reach, stacked)
    return gathered.reshape(K, frames)


def middle_plain(partial_value, band_width, precision_blocks):
    blocks, frames, width = partial_value.shape
    n_pix, n_tm = lax.axis_size("pix"), lax.axis_size("tm")
    summed = lax.psum_scatter(partial_value, "pix", scatter_dimension=0, tiled=True)
    rows = summed.transpose(0, 2, 1).reshape(K // n_pix, frames)
    moved = lax.all_to_all(rows, "tm", split_axis=0, concat_axis=1, tiled=True)
    here = moved.shape[0]
    start = (lax.axis_index("pix") * n_tm + lax.axis_index("tm")) * here
    widths = lax.dynamic_slice_in_dim(jnp.repeat(band_width, GROUP), start, here)
    nblocks = moved.shape[1] // FR
    padded = jnp.pad(moved.reshape(here, nblocks, FR), ((0, 0), (BMAX, BMAX), (0, 0)))
    filtered = jnp.zeros((here, nblocks, FR), jnp.float32)
    for d in range(2 * BMAX + 1):
        term = jnp.einsum(
            "kbf,fh->kbh", padded[:, d:d + nblocks], precision_blocks[d],
            preferred_element_type=jnp.float32,
        )
        filtered = filtered + jnp.where((abs(d - BMAX) <= widths)[:, None, None], term, 0.0)
    local = filtered.reshape(here, nblocks * FR).astype(jnp.bfloat16)
    traces = lax.all_to_all(local, "tm", split_axis=1, concat_axis=0, tiled=True)
    return lax.all_gather(traces, "pix", axis=0, tiled=True)


def shards(movie, noise_weight, footprints, block_ids, band_width, precision_blocks):
    n_pix, n_tm = lax.axis_size("pix"), lax.axis_size("tm")
    partial_value = project(movie, noise_weight, footprints, block_ids)
    fits = movie.shape[2] == FR and K % (n_pix * n_tm * LANE) == 0
    fits = fits and n_pix == SIDE * SIDE and n_tm * LANE == HALVES * CBLK
    form = middle if fits else middle_plain
    all_traces = form(partial_value, band_width, precision_blocks)
    return rebuild(movie, footprints, block_ids, all_traces)


def solution(mesh):
    return jax.shard_map(
        shards,
        mesh=mesh,
        in_specs=(
            P("pix", None, "tm"),
            P("pix", None),
            P("pix", None, None, None),
            P("pix", None),
            P(),
            P(),
        ),
        out_specs=(P("pix", "tm"), P("pix", None, "tm")),
        check_vma=False,
    )
```

time: 148 us -> 119 us (0.80)
  Pallas kernels: 139 us -> 113 us
  local copies, waits for them, and re-layouts: 7.32 us -> 5.05 us
    pallas_call x1, Pallas kernels: 104 us -> 92 us  [middle(): pl.pallas_call(functools.partial(middle_kernel, n_pix, n_tm), out_shape=j...]
    pallas_call x1, Pallas kernels: 18.5 us -> 11 us  [project(): pl.pallas_call(project_kernel, grid_spec=pltpu.PrefetchScalarGridSpec(num...]
    pallas_call x1, Pallas kernels: 17.3 us -> 10.2 us  [rebuild(): pl.pallas_call(rebuild_kernel, grid_spec=pltpu.PrefetchScalarGridSpec(num...]
    dynamic_slice x1 -> x0, local copies, waits for them, and re-layouts: 2.31 us -> none  [middle(): lax.dynamic_index_in_dim(gathered, lax.axis_index('pix'), 0, keepdims=False)]
where the time goes in v2:
time: 119 us
  Pallas kernels  113 us (95%)
  local copies, waits for them, and re-layouts  5.05 us (4%)
    pallas_call x1, Pallas kernels, middle(): pl.pallas_call(functools.partial(middle_kernel, n_pix, n_tm), out_shape=j...  92 us
    pallas_call x1, Pallas kernels, project(): pl.pallas_call(project_kernel, grid_spec=pltpu.PrefetchScalarGridSpec(num...  11 us
    pallas_call x1, Pallas kernels, rebuild(): pl.pallas_call(rebuild_kernel, grid_spec=pltpu.PrefetchScalarGridSpec(num...  10.2 us

profile of v2, /device:TPU:0, one launch (start us, length us, event | category | flops | bytes accessed | tf_op | source)
XLA Modules:
  0.0 118.9 jit_solution(6938501702824721828)
XLA Ops:
  0.6 0.8 copy.10
  1.4 0.6 reshape.21.ids_ref
  2.0 0.8 broadcast_in_dim.7
  2.8 1.9 %copy.12 = bf16[1408,128]{0,1:T(8,128)(2,1)} copy(bf16[1408,128]{1,0:T(8,128)(2,1)} %bitcast.13) | data formatting | bytes 720896 | tf_op jit(solution)/shard_map/reshape | solution.py:330
  4.7 0.2 broadcast_in_dim.8
  4.9 0.2 broadcast_in_dim.9
  5.1 0.6 dynamic-slice_bitcast_fusion.reach_ref
  5.7 11.0 %project.1.part_ref = bf16[32,128,512]{2,1,0:T(8,128)(2,1)} custom-call(s32[80]{0:T(128)} %reshape.21.ids_ref, bf16[20,128,128]{2,1,0:T(8,128)(2,1)} %movie_ref.3, f32[20,128]{1,0:T(8,128)} %noise_ref.1, bf16[20,4,128,512]{3,2,1,0:T(8,128)(2,1)} %feet_ref.3), custom_call_target="tpu_custom_call" | custom-call | tf_op jit(solution)/shard_map/project/pallas_call | solution.py:59
  16.7 92.0 %middle.1 = bf16[4,4,8,128,128]{4,3,2,1,0:T(8,128)(2,1)} custom-call(bf16[32,128,512]{2,1,0:T(8,128)(2,1)} %project.1.part_ref, s32[4,128]{1,0:T(4,128)} %dynamic-slice_bitcast_fusion.reach_ref, bf16[128,1408]{1,0:T(8,128)(2,1)} %bitcast.12), custom_call_target="tpu_custom_call" | custom-call | tf_op jit(solution)/shard_map/middle/pallas_call | solution.py:334
  108.7 10.2 %rebuild.1 = (bf16[8,512,128]{2,1,0:T(8,128)(2,1)}, bf16[20,128,128]{2,1,0:T(8,128)(2,1)}) custom-call(s32[80]{0:T(128)} %reshape.21.ids_ref, s32[1]{0:T(128)} %bitcast.me_ref, bf16[20,128,128]{2,1,0:T(8,128)(2,1)} %movie_ref.3, bf16[20,4,128,512]{3,2,1,0:T(8,128)(2,1)} %feet_ref.3, bf16[32,512,128]{2,1,0:T(8,128)(2,1)} %bitcast.11), custom_call_target="tpu_custom_call" | custom-call | tf_op jit(solution)/shard_map/rebuild/pallas_call | solution.py:111
  (1 shorter events, 0.0 us)

commit v3 on v2

--- a/solution.py
+++ b/solution.py
@@ -40,15 +40,17 @@
             for slot in range(slots)
         ]
         for slot in range(slots):
-            acc_ref[ids_ref[at * slots + slot]] += products[slot]
+            acc_ref[ids_ref[at, slot]] += products[slot]
 
     @pl.when(tile == pl.num_programs(0) - 1)
     def _():
         def put(b, carry):
-            out_ref[b] = acc_ref[b].astype(out_ref.dtype)
+            for c in range(out_ref.shape[0]):
+                span = slice(c * LANE, (c + 1) * LANE)
+                out_ref[c, b] = acc_ref[b, :, span].astype(out_ref.dtype)
             return carry
 
-        lax.fori_loop(0, out_ref.shape[0], put, 0)
+        lax.fori_loop(0, out_ref.shape[1], put, 0)
 
 
 def project(movie, noise_weight, footprints, block_ids):
@@ -56,6 +58,7 @@
     frames = movie.shape[2]
     blocks = K // CBLK
     batch = tile_batch(tiles)
+    shape = (width // LANE, blocks, frames, LANE)
     return pl.pallas_call(
         project_kernel,
         grid_spec=pltpu.PrefetchScalarGridSpec(
@@ -66,13 +69,13 @@
                 pl.BlockSpec((tiles, pixels), lambda n, ids: (0, 0)),
                 pl.BlockSpec((batch, slots, pixels, width), lambda n, ids: (n, 0, 0, 0)),
             ],
-            out_specs=pl.BlockSpec((blocks, frames, width), lambda n, ids: (0, 0, 0)),
+            out_specs=pl.BlockSpec(shape, lambda n, ids: (0, 0, 0, 0)),
             scratch_shapes=[pltpu.VMEM((blocks, frames, width), jnp.float32)],
         ),
-        out_shape=jax.ShapeDtypeStruct((blocks, frames, width), jnp.bfloat16),
+        out_shape=jax.ShapeDtypeStruct(shape, jnp.bfloat16),
         compiler_params=pltpu.CompilerParams(vmem_limit_bytes=VMEM_LIMIT),
         name="project",
-    )(block_ids.reshape(-1), movie, noise_weight, footprints)
+    )(block_ids, movie, noise_weight, footprints)
 
 
 def rebuild_kernel(ids_ref, me_ref, movie_ref, feet_ref, traces_ref, own_ref, out_ref):
@@ -94,7 +97,7 @@
         rebuilt = None
         for slot in range(slots):
             term = jnp.dot(
-                feet_ref[member, slot], traces_ref[ids_ref[at * slots + slot]],
+                feet_ref[member, slot], traces_ref[ids_ref[at, slot]],
                 preferred_element_type=jnp.float32,
             )
             rebuilt = term if rebuilt is None else rebuilt + term
@@ -130,21 +133,21 @@
         compiler_params=pltpu.CompilerParams(vmem_limit_bytes=VMEM_LIMIT),
         name="rebuild",
     )(
-        block_ids.reshape(-1), lax.axis_index("pix").reshape(1),
+        block_ids, lax.axis_index("pix").reshape(1),
         movie, footprints, traces.reshape(blocks, width, frames),
     )
     return own_traces.reshape(K // n_pix, frames), residual
 
 
 def middle_kernel(
-    n_pix, n_tm, part_ref, reach_ref, prec_ref, out_ref,
+    n_pix, n_tm, ids_ref, part_ref, reach_ref, prec_ref, movie_ref, feet_hbm,
+    traces_ref, residual_ref,
     far_buf, near_buf, hop_out, hop_in, x_buf, xt_buf, y_buf,
+    prec_t, feet_ref, total_ref,
     far_s, far_r, near_s, near_r, hop_s, hop_r,
-    a_s, a_r, b_s, b_r, g_s, g_r, relay_s, relay_r,
+    g_s, g_r, relay_s, relay_r, a_s, a_r, b_s, b_r, feet_sem, *gathered,
 ):
     chunks = far_buf.shape[0]
-    lanes = xt_buf.shape[3]
-    groups = CBLK // lanes
     parts_half = n_tm // HALVES
     me_p = lax.axis_index("pix")
     me_t = lax.axis_index("tm")
@@ -158,8 +161,10 @@
     def tm_at(e):
         return lax.rem(me_t + e, n_tm)
 
-    def part_at(owner, c, h):
-        return (owner * chunks + c) * HALVES + h
+    def part_at(owner, h):
+        return pl.ds(owner * n_tm + h * parts_half, parts_half)
+
+    load_feet = pltpu.make_async_copy(feet_hbm, feet_ref, feet_sem)
 
     barrier = pltpu.get_barrier_semaphore()
     for peer in first:
@@ -177,22 +182,22 @@
         )
 
     def far_copy(c, h):
-        source = part_ref.at[part_at(across, c, h)]
+        source = part_ref.at[c, part_at(across, h)]
         return pix_copy(source, far_buf.at[c, h], far_s, far_r, c, h, first[h])
 
     def near_copy(c, h):
-        source = part_ref.at[part_at(first[h], c, h)]
+        source = part_ref.at[c, part_at(first[h], h)]
         return pix_copy(source, near_buf.at[c, h], near_s, near_r, c, h, first[h])
 
     def hop_copy(c, h):
         return pix_copy(hop_out.at[c, h], hop_in.at[c, h], hop_s, hop_r, c, h, second[h])
 
     def g_copy(c, h):
-        rows = out_ref.at[me_p, c]
+        rows = gathered[c].at[pl.ds(me_p * n_tm, n_tm)]
         return pix_copy(rows, rows, g_s, g_r, c, h, first[h])
 
     def relay_copy(c, h):
-        rows = out_ref.at[first[h], c, pl.ds(h * parts_half, parts_half)]
+        rows = gathered[c].at[part_at(first[h], h)]
         return pix_copy(rows, rows, relay_s, relay_r, c, h, second[h])
 
     def a_copy(c, e):
@@ -210,7 +215,7 @@
         peer = tm_at(e)
         return pltpu.make_async_remote_copy(
             src_ref=y_buf.at[c, peer],
-            dst_ref=out_ref.at[me_p, c, me_t],
+            dst_ref=gathered[c].at[me_p * n_tm + me_t],
             send_sem=b_s.at[c, e - 1],
             recv_sem=b_r.at[c, e - 1],
             device_id={"tm": peer},
@@ -228,21 +233,22 @@
     def send_hop(c):
         for h in range(HALVES):
             far_copy(c, h).wait_recv()
-            total = part_ref[part_at(second[h], c, h)].astype(jnp.float32)
-            total = total + far_buf[c, h].astype(jnp.float32)
-            hop_out[c, h] = total.astype(hop_out.dtype)
+            for g in range(parts_half):
+                total = part_ref[c, second[h] * n_tm + h * parts_half + g].astype(jnp.float32)
+                total = total + far_buf[c, h, g].astype(jnp.float32)
+                hop_out[c, h, g] = total.astype(hop_out.dtype)
             hop_copy(c, h).start()
 
     def sum_chunk(c):
         for h in range(HALVES):
             near_copy(c, h).wait_recv()
             hop_copy(c, h).wait_recv()
-            for g in range(groups):
-                span = slice(g * lanes, (g + 1) * lanes)
-                total = part_ref[part_at(me_p, c, h), :, span].astype(jnp.float32)
-                total = total + near_buf[c, h, :, span].astype(jnp.float32)
-                total = total + hop_in[c, h, :, span].astype(jnp.float32)
-                x_buf[c, h * groups + g] = total.astype(x_buf.dtype)
+            for g in range(parts_half):
+                part = h * parts_half + g
+                total = part_ref[c, me_p * n_tm + part].astype(jnp.float32)
+                total = total + near_buf[c, h, g].astype(jnp.float32)
+                total = total + hop_in[c, h, g].astype(jnp.float32)
+                x_buf[c, part] = total.astype(x_buf.dtype)
         for e in range(1, n_tm):
             a_copy(c, e).start()
         xt_buf[c, me_t + BMAX] = x_buf[c, me_t]
@@ -260,7 +266,7 @@
                 [xt_buf[c, i + d + BMAX] * keep[abs(d)] for d in range(-BMAX, BMAX + 1)],
                 axis=0,
             )
-            result = jnp.dot(prec_ref[...], source, preferred_element_type=jnp.float32)
+            result = jnp.dot(prec_t[...], source, preferred_element_type=jnp.float32)
             return result.T.astype(jnp.bfloat16)
 
         def step(e, carry):
@@ -271,28 +277,65 @@
         lax.fori_loop(0, n_tm, step, 0)
         for e in range(1, n_tm):
             b_copy(c, e).start()
-        out_ref[me_p, c, me_t] = y_buf[c, me_t]
+        gathered[c][me_p * n_tm + me_t] = y_buf[c, me_t]
 
     def gather_chunk(c):
         for e in range(1, n_tm):
             b_copy(c, e).wait_recv()
         for h in range(HALVES):
             g_copy(c, h).start()
+        for j in range(n_tm):
+            traces_ref[j, c * LANE:(c + 1) * LANE, :] = gathered[c][me_p * n_tm + j]
 
     def relay_chunk(c):
         for h in range(HALVES):
             g_copy(c, h).wait_recv()
             relay_copy(c, h).start()
 
+    def rebuild_chunk(c):
+        for h in range(HALVES):
+            relay_copy(c, h).wait_recv()
+        if c == 0:
+            load_feet.wait()
+        tiles, slots = feet_ref.shape[:2]
+        span = slice(c * LANE, (c + 1) * LANE)
+
+        def one_tile(n):
+            feet = jnp.concatenate([feet_ref[n, slot, :, span] for slot in range(slots)], axis=1)
+            chosen = jnp.concatenate(
+                [gathered[c][ids_ref[n, slot]] for slot in range(slots)], axis=0
+            )
+            rebuilt = jnp.dot(feet, chosen, preferred_element_type=jnp.float32)
+            if c > 0:
+                rebuilt = rebuilt + total_ref[n]
+            if c < chunks - 1:
+                total_ref[n] = rebuilt
+            else:
+                left = movie_ref[n].astype(jnp.float32) - rebuilt
+                residual_ref[n] = left.astype(residual_ref.dtype)
+
+        batch = tile_batch(tiles)
+
+        def step(k, carry):
+            for member in range(batch):
+                one_tile(k * batch + member)
+            return carry
+
+        lax.fori_loop(0, tiles // batch, step, 0)
+
     send_far(0)
     send_near(0)
+    load_feet.start()
+    for d in range(prec_ref.shape[0]):
+        matrix = prec_ref[d].astype(jnp.float32)
+        prec_t[:, d * FR:(d + 1) * FR] = matrix.T.astype(prec_t.dtype)
     edge = jnp.zeros((BMAX,) + xt_buf.shape[2:], xt_buf.dtype)
     for c in range(chunks):
         xt_buf[c, pl.ds(0, BMAX)] = edge
         xt_buf[c, pl.ds(BMAX + n_tm, BMAX)] = edge
     if chunks > 1:
         send_far(1)
-    for t in range(chunks + 3):
+    for t in range(chunks + 4):
         if t < chunks:
             send_hop(t)
         if t + 1 < chunks:
@@ -305,12 +348,11 @@
             filter_chunk(t - 1)
         if 0 <= t - 2 < chunks:
             gather_chunk(t - 2)
-        if 0 <= t - 3:
+        if 0 <= t - 3 < chunks:
             relay_chunk(t - 3)
-
-    for c in range(chunks):
-        for h in range(HALVES):
-            relay_copy(c, h).wait_recv()
+        if 0 <= t - 4:
+            rebuild_chunk(t - 4)
+
     for c in range(chunks):
         for h in range(HALVES):
             for copy in (far_copy, near_copy, hop_copy, g_copy, relay_copy):
@@ -320,41 +362,47 @@
             b_copy(c, e).wait_send()
 
 
-def middle(partial_value, band_width, precision_blocks):
-    blocks, frames, width = partial_value.shape
+def middle(partial_value, movie, footprints, block_ids, band_width, precision_blocks):
+    chunks, blocks, frames, lanes = partial_value.shape
     n_pix, n_tm = lax.axis_size("pix"), lax.axis_size("tm")
-    chunks = K // (n_pix * n_tm * LANE)
-    reach = jnp.repeat(band_width, GROUP).reshape(n_pix, chunks, n_tm, LANE)
-    reach = lax.dynamic_index_in_dim(reach, lax.axis_index("pix"), 0, keepdims=False)
-    reach = lax.dynamic_index_in_dim(reach, lax.axis_index("tm"), 1, keepdims=False)
-    stacked = precision_blocks.reshape(-1, FR).T
+    reach = jnp.repeat(band_width.reshape(blocks, chunks, -1), GROUP, axis=2)
+    mine = lax.axis_index("pix") * n_tm + lax.axis_index("tm")
+    reach = lax.dynamic_index_in_dim(reach, mine, 0, keepdims=False)
     dma = pltpu.SemaphoreType.DMA
     bf16 = jnp.bfloat16
     vmem = pl.BlockSpec(memory_space=pltpu.VMEM)
-    gathered = pl.pallas_call(
+    part = (frames, lanes)
+    traces, residual = pl.pallas_call(
         functools.partial(middle_kernel, n_pix, n_tm),
-        out_shape=jax.ShapeDtypeStruct((n_pix, chunks, n_tm, LANE, frames), bf16),
-        in_specs=[vmem, vmem, vmem],
-        out_specs=vmem,
-        scratch_shapes=[pltpu.VMEM((chunks, HALVES, frames, width), bf16)] * 4 + [
-            pltpu.VMEM((chunks, n_tm, frames, LANE), bf16),
-            pltpu.VMEM((chunks, n_tm + 2 * BMAX, frames, LANE), bf16),
-            pltpu.VMEM((chunks, n_tm, LANE, frames), bf16),
-        ] + [dma((chunks, HALVES))] * 6 + [dma((chunks, n_tm - 1))] * 4
-        + [dma((chunks, HALVES))] * 4,
+        out_shape=[
+            jax.ShapeDtypeStruct((n_tm, CBLK, frames), bf16),
+            jax.ShapeDtypeStruct(movie.shape, bf16),
+        ],
+        in_specs=[pl.BlockSpec(memory_space=pltpu.SMEM)] + [vmem] * 4
+        + [pl.BlockSpec(memory_space=pl.ANY)],
+        out_specs=[vmem, vmem],
+        scratch_shapes=[pltpu.VMEM((chunks, HALVES, n_tm // HALVES) + part, bf16)] * 4 + [
+            pltpu.VMEM((chunks, n_tm) + part, bf16),
+            pltpu.VMEM((chunks, n_tm + 2 * BMAX) + part, bf16),
+            pltpu.VMEM((chunks, n_tm, lanes, frames), bf16),
+            pltpu.VMEM((FR, precision_blocks.shape[0] * FR), bf16),
+            pltpu.VMEM(footprints.shape, bf16),
+            pltpu.VMEM(movie.shape, jnp.float32),
+        ] + [dma((chunks, HALVES))] * 10 + [dma((chunks, n_tm - 1))] * 4 + [dma]
+        + [pltpu.VMEM((blocks, lanes, frames), bf16)] * chunks,
         compiler_params=pltpu.CompilerParams(
             collective_id=0, has_side_effects=True, vmem_limit_bytes=VMEM_LIMIT
         ),
         name="middle",
-    )(partial_value, reach, stacked)
-    return gathered.reshape(K, frames)
-
-
-def middle_plain(partial_value, band_width, precision_blocks):
-    blocks, frames, width = partial_value.shape
+    )(block_ids, partial_value, reach, precision_blocks, movie, footprints)
+    return traces.reshape(K // n_pix, frames), residual
+
+
+def middle_plain(partial_value, movie, footprints, block_ids, band_width, precision_blocks):
+    frames = movie.shape[2]
     n_pix, n_tm = lax.axis_size("pix"), lax.axis_size("tm")
-    summed = lax.psum_scatter(partial_value, "pix", scatter_dimension=0, tiled=True)
-    rows = summed.transpose(0, 2, 1).reshape(K // n_pix, frames)
+    summed = lax.psum_scatter(partial_value, "pix", scatter_dimension=1, tiled=True)
+    rows = summed.transpose(1, 0, 3, 2).reshape(K // n_pix, frames)
     moved = lax.all_to_all(rows, "tm", split_axis=0, concat_axis=1, tiled=True)
     here = moved.shape[0]
     start = (lax.axis_index("pix") * n_tm + lax.axis_index("tm")) * here
@@ -370,17 +418,16 @@
         filtered = filtered + jnp.where((abs(d - BMAX) <= widths)[:, None, None], term, 0.0)
     local = filtered.reshape(here, nblocks * FR).astype(jnp.bfloat16)
     traces = lax.all_to_all(local, "tm", split_axis=1, concat_axis=0, tiled=True)
-    return lax.all_gather(traces, "pix", axis=0, tiled=True)
+    gathered = lax.all_gather(traces, "pix", axis=0, tiled=True)
+    return rebuild(movie, footprints, block_ids, gathered)
 
 
 def shards(movie, noise_weight, footprints, block_ids, band_width, precision_blocks):
     n_pix, n_tm = lax.axis_size("pix"), lax.axis_size("tm")
     partial_value = project(movie, noise_weight, footprints, block_ids)
-    fits = movie.shape[2] == FR and K % (n_pix * n_tm * LANE) == 0
-    fits = fits and n_pix == SIDE * SIDE and n_tm * LANE == HALVES * CBLK
+    fits = movie.shape[2] == FR and n_pix == SIDE * SIDE and n_pix * n_tm == K // CBLK
     form = middle if fits else middle_plain
-    all_traces = form(partial_value, band_width, precision_blocks)
-    return rebuild(movie, footprints, block_ids, all_traces)
+    return form(partial_value, movie, footprints, block_ids, band_width, precision_blocks)
 
 
 def solution(mesh):

time: 119 us -> 113 us (0.950)
  Pallas kernels: 113 us -> 104 us
  local copies, waits for them, and re-layouts: 5.05 us -> 7.35 us
    pallas_call x2 -> x1, Pallas kernels: 102 us -> 93.1 us  [middle(): pl.pallas_call(functools.partial(middle_kernel, n_pix, n_tm), out_shape=[...]
    unnamed x1 -> x3, local copies, waits for them, and re-layouts: 0.77 us -> 5.61 us
    reshape x2, local copies, waits for them, and re-layouts: 2.51 us -> 0.88 us  [middle(): reach = jnp.repeat(band_width.reshape(blocks, chunks, -1), GROUP, axis=2)]
where the time goes in v3:
time: 113 us; the launch traced here: 112 us
  Pallas kernels  104 us (92%)
  local copies, waits for them, and re-layouts  7.35 us (7%)
    pallas_call x1, Pallas kernels, middle(): pl.pallas_call(functools.partial(middle_kernel, n_pix, n_tm), out_shape=[...  93.1 us
    pallas_call x1, Pallas kernels, project(): pl.pallas_call(project_kernel, grid_spec=pltpu.PrefetchScalarGridSpec(num...  11.3 us
    unnamed x3, local copies, waits for them, and re-layouts  5.61 us

profile of v3, /device:TPU:0, one launch (start us, length us, event | category | flops | bytes accessed | tf_op | source)
XLA Modules:
  0.0 112.4 jit_solution(6353340863333140712)
XLA Ops:
  0.6 1.4 %copy.15.ids_ref = s32[20,4]{1,0:T(8,128)} copy(s32[20,4]{0,1:T(4,128)} %param.9) | data formatting | bytes 640 | tf_op args[3]
  2.0 0.8 reshape.13
  2.8 0.1 copy.14
  2.9 0.8 dynamic-slice_reduce_fusion.reach_ref
  3.8 11.3 %project.1.part_ref = bf16[4,32,128,128]{3,2,1,0:T(8,128)(2,1)} custom-call(s32[20,4]{1,0:T(8,128)} %copy.15.ids_ref, bf16[20,128,128]{2,1,0:T(8,128)(2,1)} %movie_ref.3, f32[20,128]{1,0:T(8,128)} %noise_ref.1, bf16[20,4,128,512]{3,2,1,0:T(8,128)(2,1)} %feet_hbm.1), custom_call_target="tpu_custom_call" | custom-call | tf_op jit(solution)/shard_map/project/pallas_call | solution.py:62
  15.0 93.1 %middle.1 = (bf16[8,512,128]{2,1,0:T(8,128)(2,1)}, bf16[20,128,128]{2,1,0:T(8,128)(2,1)}) custom-call(s32[20,4]{1,0:T(8,128)} %copy.15.ids_ref, bf16[4,32,128,128]{3,2,1,0:T(8,128)(2,1)} %project.1.part_ref, s32[4,128]{1,0:T(4,128)} %dynamic-slice_reduce_fusion.reach_ref, bf16[11,128,128]{2,1,0:T(8,128)(2,1)} %prec_ref.1, bf16[20,128,128]{2,1,0:T(8,128)(2,1)} %movie_ref.3, ...), custom_call_target="tpu_custom_call" | custom-call | tf_op jit(solution)/shard_map/middle/pallas_call | solution.py:375
  108.1 2.3 %copy.18 = bf16[4096,128]{1,0:T(8,128)(2,1)} copy(bf16[4096,128]{1,0:T(8,128)(2,1)} %bitcast.2) | data formatting | bytes 2097152
  110.4 2.0 %copy.19 = bf16[20,128,128]{2,1,0:T(8,128)(2,1)} copy(bf16[20,128,128]{2,1,0:T(8,128)(2,1)} %get-tuple-element.9) | data formatting | bytes 1310720
  (1 shorter events, 0.0 us)

commit v4 on v3

--- a/solution.py
+++ b/solution.py
@@ -344,11 +344,15 @@
             send_far(t + 2)
         if t < chunks:
             sum_chunk(t)
+            if t >= 2:
+                gather_chunk(t - 2)
+            if t >= 3:
+                relay_chunk(t - 3)
         if 0 <= t - 1 < chunks:
             filter_chunk(t - 1)
-        if 0 <= t - 2 < chunks:
+        if t >= chunks and 0 <= t - 2 < chunks:
             gather_chunk(t - 2)
-        if 0 <= t - 3 < chunks:
+        if t >= chunks and 0 <= t - 3 < chunks:
             relay_chunk(t - 3)
         if 0 <= t - 4:
             rebuild_chunk(t - 4)

time: 113 us -> 112 us (level)
  no operation moved by 1% of the time
where the time goes in v4:
time: 112 us; the launch traced here: 111 us
  Pallas kernels  103 us (92%)
  local copies, waits for them, and re-layouts  7.35 us (7%)
    pallas_call x1, Pallas kernels, middle(): pl.pallas_call(functools.partial(middle_kernel, n_pix, n_tm), out_shape=[...  92 us
    pallas_call x1, Pallas kernels, project(): pl.pallas_call(project_kernel, grid_spec=pltpu.PrefetchScalarGridSpec(num...  11.3 us
    unnamed x3, local copies, waits for them, and re-layouts  5.61 us

profile of v4, /device:TPU:0, one launch (start us, length us, event | category | flops | bytes accessed | tf_op | source)
XLA Modules:
  0.0 111.3 jit_solution(16699910165781780365)
XLA Ops:
  0.6 1.4 %copy.15.ids_ref = s32[20,4]{1,0:T(8,128)} copy(s32[20,4]{0,1:T(4,128)} %param.9) | data formatting | bytes 640 | tf_op args[3]
  2.0 0.8 reshape.13
  2.8 0.1 copy.14
  2.9 0.8 dynamic-slice_reduce_fusion.reach_ref
  3.8 11.3 %project.1.part_ref = bf16[4,32,128,128]{3,2,1,0:T(8,128)(2,1)} custom-call(s32[20,4]{1,0:T(8,128)} %copy.15.ids_ref, bf16[20,128,128]{2,1,0:T(8,128)(2,1)} %movie_ref.3, f32[20,128]{1,0:T(8,128)} %noise_ref.1, bf16[20,4,128,512]{3,2,1,0:T(8,128)(2,1)} %feet_hbm.1), custom_call_target="tpu_custom_call" | custom-call | tf_op jit(solution)/shard_map/project/pallas_call | solution.py:62
  15.0 92.0 %middle.1 = (bf16[8,512,128]{2,1,0:T(8,128)(2,1)}, bf16[20,128,128]{2,1,0:T(8,128)(2,1)}) custom-call(s32[20,4]{1,0:T(8,128)} %copy.15.ids_ref, bf16[4,32,128,128]{3,2,1,0:T(8,128)(2,1)} %project.1.part_ref, s32[4,128]{1,0:T(4,128)} %dynamic-slice_reduce_fusion.reach_ref, bf16[11,128,128]{2,1,0:T(8,128)(2,1)} %prec_ref.1, bf16[20,128,128]{2,1,0:T(8,128)(2,1)} %movie_ref.3, ...), custom_call_target="tpu_custom_call" | custom-call | tf_op jit(solution)/shard_map/middle/pallas_call | solution.py:379
  107.1 2.3 %copy.18 = bf16[4096,128]{1,0:T(8,128)(2,1)} copy(bf16[4096,128]{1,0:T(8,128)(2,1)} %bitcast.2) | data formatting | bytes 2097152
  109.3 2.0 %copy.19 = bf16[20,128,128]{2,1,0:T(8,128)(2,1)} copy(bf16[20,128,128]{2,1,0:T(8,128)(2,1)} %get-tuple-element.9) | data formatting | bytes 1310720
  (1 shorter events, 0.0 us)
